TPU v7x, 256 devices: a whole 4x4x8 slice. The times are simulated.
256 devices in a mesh: row: 16 (over z, core), col: 16 (over x, y).
Axes of the slice: x: 4, y: 4, z: 8, core: 2. Of those that a mesh axis runs over, the one named last changes fastest.
Arguments:
- token_ids: int32 [32, 256], P('row'), may hold values from 0 to 16383
- passage_lengths: int32 [32], P('row'), may hold values from 64 to 256, as said below
- embedding: bfloat16 [16384, 4096], P(None, 'col'), may hold values from -8 to 8
- attn_gain: bfloat16 [4096], P('col'), may hold values from 0.25 to 1.75
- final_gain: bfloat16 [4096], P('col'), may hold values from 0.25 to 1.75
- query_weight: bfloat16 [4096, 4096], P('row', 'col'), may hold values from -0.5 to 0.5
- key_weight: bfloat16 [4096, 4096], P('row', 'col'), may hold values from -0.5 to 0.5
- value_weight: bfloat16 [4096, 4096], P('row', 'col'), may hold values from -0.09375 to 0.09375
- out_weight: bfloat16 [4096, 4096], P('row', 'col'), may hold values from -0.09375 to 0.09375
- crosskey_weight: bfloat16 [4096, 4096], P('row', 'col'), may hold values from -0.09375 to 0.09375
- crossvalue_weight: bfloat16 [4096, 4096], P('row', 'col'), may hold values from -0.09375 to 0.09375
Outputs:
- hidden_out: bfloat16 [8192, 4096], P('row', 'col')
- cross_keys: bfloat16 [8192, 16, 256], P('row', 'col')
- cross_values: bfloat16 [8192, 16, 256], P('row', 'col')
Inputs may be any that keep to these rules, and one draw needn't show every extreme that they name: `passage_lengths`: some passage of every draw has all 256 slots valid.
All inputs are finite; a program needn't handle non-finite values.
Results may differ from a plain program's by a relative error of at most 0.0082.
Values may be sent and summed in bfloat16 or wider, within the bound.
No kernel may reach another device: no remote copies, remote signals or barrier semaphores. Data moves between devices by JAX's collectives and lax.ppermute only.
A program may use at most 64 MiB of HBM per device.

v0:
```python
import jax
import jax.numpy as jnp
from jax import lax
from jax.sharding import PartitionSpec as P

D = 4096
HD = 256
PLEN = 256
epsilon = 1e-06
masked_score = -1000000000.0


def scaled_rows(widened, summed, gain_row):
    inverse = lax.rsqrt(summed / D + epsilon)
    return (widened * inverse * gain_row.astype(jnp.float32)).astype(jnp.bfloat16)


def spread_norm(row_block, gain_row, which):
    widened = row_block.astype(jnp.float32)
    partial_sum = jnp.sum(widened * widened, axis=1, keepdims=True)
    if which == 0:
        summed = lax.psum(partial_sum, "col")
        return lax.all_gather(
            scaled_rows(widened, summed, gain_row[None, :]), "col", axis=1, tiled=True
        )
    else:
        summed = lax.psum(partial_sum, "col")
        return lax.all_gather(
            scaled_rows(widened, summed, gain_row[None, :]), "col", axis=1, tiled=True
        )


def add_terms(source, pieces):
    return tuple(
        (
            jnp.dot(source, weight_piece, preferred_element_type=jnp.float32)
            for weight_piece in pieces
        )
    )


def attend(query_rows, key_rows, value_rows, passage_lengths):
    tok_rows, local_width = query_rows.shape
    passages_here = tok_rows // PLEN
    heads_here = local_width // HD
    query_four = query_rows.reshape(passages_here, PLEN, heads_here, HD)
    key_four = key_rows.reshape(passages_here, PLEN, heads_here, HD)
    value_four = value_rows.reshape(passages_here, PLEN, heads_here, HD)
    scores = jnp.einsum(
        "pihd,pjhd->phij", query_four, key_four, preferred_element_type=jnp.float32
    ) * HD ** (-0.5)
    valid = jnp.arange(PLEN, dtype=jnp.int32)[None, :] < passage_lengths[:, None]
    scores = jnp.where(valid[:, None, None, :], scores, masked_score)
    highest = jnp.max(scores, axis=-1, keepdims=True)
    expon = jnp.exp(scores - highest)
    probs = (expon / jnp.sum(expon, axis=-1, keepdims=True)).astype(jnp.bfloat16)
    mixed = jnp.einsum("phij,pjhd->pihd", probs, value_four, preferred_element_type=jnp.float32)
    return mixed.astype(jnp.bfloat16).reshape(tok_rows, local_width)


def shards(
    token_ids,
    passage_lengths,
    embedding,
    attn_gain,
    final_gain,
    query_weight,
    key_weight,
    value_weight,
    out_weight,
    crosskey_weight,
    crossvalue_weight,
):
    embedded = jnp.take(embedding, token_ids.reshape(-1), axis=0)
    normed = spread_norm(embedded, attn_gain, 0)
    tok_rows = normed.shape[0]
    local_width = query_weight.shape[1]
    query_sum, key_sum, value_sum = add_terms(
        normed,
        (
            lax.all_gather(query_weight, "row", axis=0, tiled=True),
            lax.all_gather(key_weight, "row", axis=0, tiled=True),
            lax.all_gather(value_weight, "row", axis=0, tiled=True),
        ),
    )
    attended = attend(
        query_sum.astype(jnp.bfloat16),
        key_sum.astype(jnp.bfloat16),
        value_sum.astype(jnp.bfloat16),
        passage_lengths,
    )
    heads_full = lax.all_gather(attended, "col", axis=1, tiled=True)
    (projected,) = add_terms(heads_full, (lax.all_gather(out_weight, "row", axis=0, tiled=True),))
    hidden_out = (embedded.astype(jnp.float32) + projected).astype(jnp.bfloat16)
    final_normed = spread_norm(hidden_out, final_gain, 1)
    crosskey_sum, crossvalue_sum = add_terms(
        final_normed,
        (
            lax.all_gather(crosskey_weight, "row", axis=0, tiled=True),
            lax.all_gather(crossvalue_weight, "row", axis=0, tiled=True),
        ),
    )
    heads_here = local_width // HD
    cross_keys = crosskey_sum.astype(jnp.bfloat16).reshape(tok_rows, heads_here, HD)
    cross_values = crossvalue_sum.astype(jnp.bfloat16).reshape(tok_rows, heads_here, HD)
    return (hidden_out, cross_keys, cross_values)


def solution(mesh):
    return jax.shard_map(
        shards,
        mesh=mesh,
        in_specs=(
            P("row", None),
            P("row"),
            P(None, "col"),
            P("col"),
            P("col"),
            P("row", "col"),
            P("row", "col"),
            P("row", "col"),
            P("row", "col"),
            P("row", "col"),
            P("row", "col"),
        ),
        out_specs=(P("row", "col"), P("row", "col", None), P("row", "col", None)),
        check_vma=False,
    )
```

profile of v0, /device:TPU:1, one launch (start us, length us, event | category | flops | bytes accessed | tf_op | source)
XLA Modules:
  0.0 447.0 jit_solution(17359749313425114075)
XLA Ops:
  7.2 0.0 copy-start
  7.2 0.0 all-gather.14.cloned.1.call-start
  7.2 0.7 all-gather.14.cloned.1.call-update
  7.9 0.0 all-gather.10.cloned.1.call-start
  8.0 0.7 convert_element_type.53
  8.6 0.7 copy.22
  9.3 6.0 %gather_fusion = bf16[512,256]{1,0:T(8,128)(2,1)S(1)} fusion(bf16[16384,256]{1,0:T(8,128)(2,1)} %param.13, s32[1024]{0:T(1024)S(1)} %pad_clamp_fusion), kind=kCustom, calls=%fused_computation | custom fusion | bytes 526336 | tf_op jit(solution)/shard_map/jit(_take)/gather | solution.py:74
  15.4 0.1 copy.17
  15.5 0.1 fusion.10
  15.6 34.2 %psum.14 = f32[512,1]{0,1:T(1,128)S(1)} all-reduce(f32[512,1]{0,1:T(1,128)S(1)} %bitcast.48), channel_id=1, replica_groups=mesh['row'=16,'col'=16] {'col'}, use_global_device_ids=true, to_apply=%region_1.2 | all-reduce | flops 512 | bytes 4096 | tf_op jit(solution)/shard_map/psum | solution.py:22
  49.9 0.8 fusion.12
  50.7 0.0 all-gather.10.cloned.1.call-update
  50.7 0.0 all-gather.16.cloned.1.call-start
  50.8 0.7 all-gather.16.cloned.1.call-update
  51.5 0.0 all-gather.12.cloned.1.call-start
  51.5 0.5 all-gather.12.cloned.1.call-update
  52.0 0.0 all-gather.20.cloned.1.call-start
  52.1 0.5 all-gather.20.cloned.1.call-update
  52.6 0.0 all-gather.18.cloned.1.call-start
  52.7 0.1 iota_compare_fusion
  52.8 0.7 all-gather.14.cloned.1.call-done
  53.5 58.8 %all-gather.10.cloned.1.call-done = bf16[512,4096]{0,1:T(8,128)(2,1)} async-done(((bf16[512,256]{0,1:T(8,128)(2,1)}), bf16[512,4096]{0,1:T(8,128)(2,1)}) %all-gather.10.cloned.1.call-update) | async-done | bytes 4194320 | tf_op jit(solution)/shard_map/all_gather | solution.py:23
  112.3 4.2 convolution_convert_fusion.4
  116.4 37.4 %all-gather.16.cloned.1.call-done = bf16[4096,256]{1,0:T(8,128)(2,1)} async-done(((bf16[256,256]{1,0:T(8,128)(2,1)}), bf16[4096,256]{1,0:T(8,128)(2,1)}) %all-gather.16.cloned.1.call-update) | async-done | bytes 2097168 | tf_op jit(solution)/shard_map/all_gather | solution.py:82
  153.9 4.2 convolution_convert_fusion.3
  158.0 0.4 fusion.15
  158.4 0.3 fusion.3
  158.7 34.7 %all-gather.12.cloned.1.call-done = bf16[4096,256]{1,0:T(8,128)(2,1)} async-done(((bf16[256,256]{1,0:T(8,128)(2,1)}), bf16[4096,256]{1,0:T(8,128)(2,1)}) %all-gather.12.cloned.1.call-update) | async-done | bytes 2097168 | tf_op jit(solution)/shard_map/all_gather | solution.py:83
  193.4 4.2 convolution_convert_fusion.5
  197.6 1.0 convolution_convert_fusion.2
  198.6 0.0 all-gather.18.cloned.1.call-update
  198.6 0.0 all-gather.24.cloned.1.call-start
  198.7 0.7 all-gather.24.cloned.1.call-update
  199.4 0.0 all-gather.22.cloned.1.call-start
  199.5 33.5 %all-gather.20.cloned.1.call-done = bf16[4096,256]{1,0:T(8,128)(2,1)} async-done(((bf16[256,256]{1,0:T(8,128)(2,1)}), bf16[4096,256]{1,0:T(8,128)(2,1)}) %all-gather.20.cloned.1.call-update) | async-done | bytes 2097168 | tf_op jit(solution)/shard_map/all_gather | solution.py:93
  232.9 61.3 %all-gather.18.cloned.1.call-done = bf16[512,4096]{1,0:T(8,128)(2,1)} async-done(((bf16[512,256]{1,0:T(8,128)(2,1)}), bf16[512,4096]{1,0:T(8,128)(2,1)}) %all-gather.18.cloned.1.call-update) | async-done | bytes 4194320 | tf_op jit(solution)/shard_map/all_gather | solution.py:92
  294.2 4.2 fusion.7
  298.4 31.3 %psum.15 = f32[512,1]{0,1:T(1,128)S(1)} all-reduce(f32[512,1]{0,1:T(1,128)S(1)} %bitcast.54), channel_id=1, replica_groups=mesh['row'=16,'col'=16] {'col'}, use_global_device_ids=true, to_apply=%region_5.6 | all-reduce | flops 512 | bytes 4096 | tf_op jit(solution)/shard_map/psum | solution.py:27
  329.7 0.8 fusion.9
  330.5 0.0 all-gather.22.cloned.1.call-update
  330.5 0.0 all-gather.26.cloned.1.call-start
  330.6 0.7 all-gather.26.cloned.1.call-update
  331.3 0.8 copy.19
  332.1 4.6 %all-gather.24.cloned.1.call-done = bf16[4096,256]{1,0:T(8,128)(2,1)} async-done(((bf16[256,256]{1,0:T(8,128)(2,1)}), bf16[4096,256]{1,0:T(8,128)(2,1)}) %all-gather.24.cloned.1.call-update) | async-done | bytes 2097168 | tf_op jit(solution)/shard_map/all_gather | solution.py:99
  336.7 57.3 %all-gather.22.cloned.1.call-done = bf16[512,4096]{0,1:T(8,128)(2,1)} async-done(((bf16[512,256]{0,1:T(8,128)(2,1)}), bf16[512,4096]{0,1:T(8,128)(2,1)}) %all-gather.22.cloned.1.call-update) | async-done | bytes 4194320 | tf_op jit(solution)/shard_map/all_gather | solution.py:28
  394.0 4.9 %fusion.5 = bf16[512,1,256]{2,0,1:T(8,128)(2,1)} fusion(bf16[512,4096]{0,1:T(8,128)(2,1)} %all-gather.22.cloned.1.call-done, bf16[4096,256]{1,0:T(8,128)(2,1)} %all-gather.24.cloned.1.call-done), kind=kOutput, calls=%fused_computation.14 | convolution fusion | flops 1073872896 | bytes 6553600 | tf_op jit(solution)/shard_map/dot_general | solution.py:36
  398.8 36.7 %all-gather.26.cloned.1.call-done = bf16[4096,256]{1,0:T(8,128)(2,1)} async-done(((bf16[256,256]{1,0:T(8,128)(2,1)}), bf16[4096,256]{1,0:T(8,128)(2,1)}) %all-gather.26.cloned.1.call-update) | async-done | bytes 2097168 | tf_op jit(solution)/shard_map/all_gather | solution.py:100
  435.6 4.9 %fusion.6 = bf16[512,1,256]{2,0,1:T(8,128)(2,1)} fusion(bf16[512,4096]{0,1:T(8,128)(2,1)} %all-gather.22.cloned.1.call-done, bf16[4096,256]{1,0:T(8,128)(2,1)} %all-gather.26.cloned.1.call-done), kind=kOutput, calls=%fused_computation.15 | convolution fusion | flops 1073872896 | bytes 6553600 | tf_op jit(solution)/shard_map/dot_general | solution.py:36
  (12 shorter events, 0.1 us)
Async XLA Ops:
  7.2 8.3 %copy-start = (s32[2,256]{1,0:T(2,128)S(1)}, s32[2,256]{1,0:T(2,128)}, u32[]{:S(2)}) copy-start(s32[2,256]{1,0:T(2,128)} %param.11) | copy-start | bytes 6148
  7.2 46.3 %all-gather.14.cloned.1.call-start = ((), (), s32[]{:S(2)}) async-start(), calls=%async_computation.2 | async-start | bytes 2228224 | tf_op jit(solution)/shard_map/all_gather | solution.py:81
  7.9 104.3 %all-gather.10.cloned.1.call-start = ((), (), s32[]{:S(2)}) async-start(), calls=%async_computation | async-start | bytes 4456448 | tf_op jit(solution)/shard_map/all_gather | solution.py:23
  9.3 43.4 %copy-start.1 = (s32[2]{0:T(128)S(1)}, s32[2]{0:T(128)}, u32[]{:S(2)}) copy-start(s32[2]{0:T(128)} %param.12) | copy-start | bytes 28
  50.7 103.1 %all-gather.16.cloned.1.call-start = ((), (), s32[]{:S(2)}) async-start(), calls=%async_computation.3 | async-start | bytes 2228224 | tf_op jit(solution)/shard_map/all_gather | solution.py:82
  51.5 141.9 %all-gather.12.cloned.1.call-start = ((), (), s32[]{:S(2)}) async-start(), calls=%async_computation.1 | async-start | bytes 2228224 | tf_op jit(solution)/shard_map/all_gather | solution.py:83
  52.0 180.9 %all-gather.20.cloned.1.call-start = ((), (), s32[]{:S(2)}) async-start(), calls=%async_computation.5 | async-start | bytes 2228224 | tf_op jit(solution)/shard_map/all_gather | solution.py:93
  52.6 241.6 %all-gather.18.cloned.1.call-start = ((), (), s32[]{:S(2)}) async-start(), calls=%async_computation.4 | async-start | bytes 4456448 | tf_op jit(solution)/shard_map/all_gather | solution.py:92
  197.6 1.9 copy-start.2
  198.6 138.1 %all-gather.24.cloned.1.call-start = ((), (), s32[]{:S(2)}) async-start(), calls=%async_computation.7 | async-start | bytes 2228224 | tf_op jit(solution)/shard_map/all_gather | solution.py:99
  199.4 194.6 %all-gather.22.cloned.1.call-start = ((), (), s32[]{:S(2)}) async-start(), calls=%async_computation.6 | async-start | bytes 4456448 | tf_op jit(solution)/shard_map/all_gather | solution.py:28
  330.5 105.1 %all-gather.26.cloned.1.call-start = ((), (), s32[]{:S(2)}) async-start(), calls=%async_computation.8 | async-start | bytes 2228224 | tf_op jit(solution)/shard_map/all_gather | solution.py:100
Sparse Core Ops, SparseCore 0:
  9.8 43.6 all-gather.13
  56.5 55.7 all-gather.9
  114.1 39.7 all-gather.15
  155.5 37.8 all-gather.11
  195.1 37.8 all-gather.19
  235.7 58.4 all-gather.17
  296.0 40.6 all-gather.23
  339.7 54.2 all-gather.21
  395.8 39.7 all-gather.25
where the time goes:
time: 447 us
  waiting for transfers between devices  329 us (74%)
  blocking collectives  65.5 us (15%)
  matrix products  28.1 us (6%)
  between operations  14 us (3%)
  local copies, waits for them, and re-layouts  7.71 us (2%)
    all_gather x2, waiting for transfers between devices, spread_norm(): lax.all_gather(scaled_rows(widened, summed, gain_row[None, :]), 'col', ax...  116 us
    psum x2, blocking collectives, spread_norm(): summed = lax.psum(partial_sum, 'col')  65.5 us
    all_gather x1, waiting for transfers between devices, shards(): heads_full = lax.all_gather(attended, 'col', axis=1, tiled=True)  61.3 us
    all_gather x1, waiting for transfers between devices, shards(): lax.all_gather(key_weight, 'row', axis=0, tiled=True)  37.4 us
    all_gather x1, waiting for transfers between devices, shards(): lax.all_gather(crossvalue_weight, 'row', axis=0, tiled=True)  36.7 us
    all_gather x1, waiting for transfers between devices, shards(): lax.all_gather(value_weight, 'row', axis=0, tiled=True)  34.7 us
    all_gather x1, waiting for transfers between devices, shards(): lax.all_gather(out_weight, 'row', axis=0, tiled=True)  33.5 us
    dot_general x6, matrix products, add_terms(): jnp.dot(source, weight_piece, preferred_element_type=jnp.float32)  26.4 us
  transfers between devices with their start and end apart: 9, of which 9 were waited for; matrix products, arithmetic and copies ran while one was open for 7% of the time, Pallas kernels for 0%

commit v1 on v0

--- a/solution.py
+++ b/solution.py
@@ -8,6 +8,15 @@
 PLEN = 256
 epsilon = 1e-06
 masked_score = -1000000000.0
+
+
+def doubling_sum(x, mesh_axis):
+    size = lax.axis_size(mesh_axis)
+    total, far = (x, 1)
+    while far < size:
+        total = total + lax.ppermute(total, mesh_axis, [(i, i ^ far) for i in range(size)])
+        far = 2 * far
+    return total
 
 
 def scaled_rows(widened, summed, gain_row):
@@ -24,7 +33,7 @@
             scaled_rows(widened, summed, gain_row[None, :]), "col", axis=1, tiled=True
         )
     else:
-        summed = lax.psum(partial_sum, "col")
+        summed = doubling_sum(partial_sum, "col")
         return lax.all_gather(
             scaled_rows(widened, summed, gain_row[None, :]), "col", axis=1, tiled=True
         )

time: 447 us -> 447 us (level)
  blocking collectives: 65.5 us -> 34.2 us
  waiting for transfers between devices: 329 us -> 354 us
  starting transfers between devices: 0.35 us -> 6.37 us
    psum x2 -> x1, blocking collectives: 65.5 us -> 34.2 us  [spread_norm(): summed = lax.psum(partial_sum, 'col')]
    all_gather x1, waiting for transfers between devices: 4.6 us -> 23 us  [shards(): lax.all_gather(crosskey_weight, 'row', axis=0, tiled=True)]
    ppermute x0 -> x4, waiting for transfers between devices: none -> 6.99 us  [doubling_sum(): lax.ppermute(total, mesh_axis, [(i, i ^ far) for i in range(size)])]
    ppermute x0 -> x4, starting transfers between devices: none -> 5.84 us  [doubling_sum(): lax.ppermute(total, mesh_axis, [(i, i ^ far) for i in range(size)])]
  transfers between devices with their start and end apart: 9 -> 13, of which waited for: 9 -> 13; matrix products, arithmetic and copies ran while one was open for 7% -> 7% of each run, Pallas kernels for 0% -> 0%
where the time goes in v1:
time: 447 us
  waiting for transfers between devices  354 us (79%)
  blocking collectives  34.2 us (8%)
  matrix products  28.1 us (6%)
  between operations  14 us (3%)
  local copies, waits for them, and re-layouts  7.71 us (2%)
  starting transfers between devices  6.37 us (1%)
    all_gather x2, waiting for transfers between devices, spread_norm(): lax.all_gather(scaled_rows(widened, summed, gain_row[None, :]), 'col', ax...  116 us
    all_gather x1, waiting for transfers between devices, shards(): heads_full = lax.all_gather(attended, 'col', axis=1, tiled=True)  61.3 us
    all_gather x1, waiting for transfers between devices, shards(): lax.all_gather(key_weight, 'row', axis=0, tiled=True)  37.4 us
    all_gather x1, waiting for transfers between devices, shards(): lax.all_gather(crossvalue_weight, 'row', axis=0, tiled=True)  36.7 us
    all_gather x1, waiting for transfers between devices, shards(): lax.all_gather(value_weight, 'row', axis=0, tiled=True)  34.7 us
    psum x1, blocking collectives, spread_norm(): summed = lax.psum(partial_sum, 'col')  34.2 us
    all_gather x1, waiting for transfers between devices, shards(): lax.all_gather(out_weight, 'row', axis=0, tiled=True)  33.5 us
    dot_general x6, matrix products, add_terms(): jnp.dot(source, weight_piece, preferred_element_type=jnp.float32)  26.4 us
  transfers between devices with their start and end apart: 13, of which 13 were waited for; matrix products, arithmetic and copies ran while one was open for 7% of the time, Pallas kernels for 0%

profile of v1, /device:TPU:1, one launch (start us, length us, event | category | flops | bytes accessed | tf_op | source)
XLA Modules:
  0.0 447.0 jit_solution(3055371866286816190)
XLA Ops:
  7.2 0.7 all-gather.14.cloned.1.call-update
  7.9 0.0 all-gather.10.cloned.1.call-start
  8.0 0.7 convert_element_type.53
  8.6 0.7 copy.22
  9.3 6.0 %gather_fusion = bf16[512,256]{1,0:T(8,128)(2,1)S(1)} fusion(bf16[16384,256]{1,0:T(8,128)(2,1)} %param.13, s32[1024]{0:T(1024)S(1)} %pad_clamp_fusion), kind=kCustom, calls=%fused_computation | custom fusion | bytes 526336 | tf_op jit(solution)/shard_map/jit(_take)/gather | solution.py:83
  15.4 0.1 copy.17
  15.5 0.1 fusion.10
  15.6 34.2 %psum.7 = f32[512,1]{0,1:T(1,128)S(1)} all-reduce(f32[512,1]{0,1:T(1,128)S(1)} %bitcast.48), channel_id=1, replica_groups=mesh['row'=16,'col'=16] {'col'}, use_global_device_ids=true, to_apply=%region_1.2 | all-reduce | flops 512 | bytes 4096 | tf_op jit(solution)/shard_map/psum | solution.py:31
  49.9 0.8 fusion.12
  50.7 0.0 all-gather.16.cloned.1.call-start
  50.8 0.7 all-gather.16.cloned.1.call-update
  51.5 0.5 all-gather.12.cloned.1.call-update
  52.0 0.0 all-gather.20.cloned.1.call-start
  52.1 0.5 all-gather.20.cloned.1.call-update
  52.6 0.0 all-gather.18.cloned.1.call-start
  52.7 0.1 iota_compare_fusion
  52.8 0.7 all-gather.14.cloned.1.call-done
  53.5 58.8 %all-gather.10.cloned.1.call-done = bf16[512,4096]{0,1:T(8,128)(2,1)} async-done(((bf16[512,256]{0,1:T(8,128)(2,1)}), bf16[512,4096]{0,1:T(8,128)(2,1)}) %all-gather.10.cloned.1.call-update) | async-done | bytes 4194320 | tf_op jit(solution)/shard_map/all_gather | solution.py:32
  112.3 4.2 convolution_convert_fusion.4
  116.4 37.4 %all-gather.16.cloned.1.call-done = bf16[4096,256]{1,0:T(8,128)(2,1)} async-done(((bf16[256,256]{1,0:T(8,128)(2,1)}), bf16[4096,256]{1,0:T(8,128)(2,1)}) %all-gather.16.cloned.1.call-update) | async-done | bytes 2097168 | tf_op jit(solution)/shard_map/all_gather | solution.py:91
  153.9 4.2 convolution_convert_fusion.3
  158.0 0.4 fusion.15
  158.4 0.3 fusion.3
  158.7 34.7 %all-gather.12.cloned.1.call-done = bf16[4096,256]{1,0:T(8,128)(2,1)} async-done(((bf16[256,256]{1,0:T(8,128)(2,1)}), bf16[4096,256]{1,0:T(8,128)(2,1)}) %all-gather.12.cloned.1.call-update) | async-done | bytes 2097168 | tf_op jit(solution)/shard_map/all_gather | solution.py:92
  193.4 4.2 convolution_convert_fusion.5
  197.6 1.0 convolution_convert_fusion.2
  198.6 0.0 all-gather.24.cloned.1.call-start
  198.7 0.7 all-gather.24.cloned.1.call-update
  199.4 33.5 %all-gather.20.cloned.1.call-done = bf16[4096,256]{1,0:T(8,128)(2,1)} async-done(((bf16[256,256]{1,0:T(8,128)(2,1)}), bf16[4096,256]{1,0:T(8,128)(2,1)}) %all-gather.20.cloned.1.call-update) | async-done | bytes 2097168 | tf_op jit(solution)/shard_map/all_gather | solution.py:102
  232.9 61.3 %all-gather.18.cloned.1.call-done = bf16[512,4096]{1,0:T(8,128)(2,1)} async-done(((bf16[512,256]{1,0:T(8,128)(2,1)}), bf16[512,4096]{1,0:T(8,128)(2,1)}) %all-gather.18.cloned.1.call-update) | async-done | bytes 4194320 | tf_op jit(solution)/shard_map/all_gather | solution.py:101
  294.2 4.2 fusion.7
  298.4 1.0 collective-permute-start
  299.4 1.5 collective-permute-done
  300.9 1.8 collective-permute-start.1
  302.8 2.1 collective-permute-done.1
  304.9 0.9 collective-permute-start.2
  305.8 1.5 collective-permute-done.2
  307.3 2.1 collective-permute-start.3
  309.4 1.8 collective-permute-done.3
  311.3 0.8 fusion.9
  312.1 0.2 all-gather.26.cloned.1.call-start
  312.3 0.5 all-gather.26.cloned.1.call-update
  312.8 0.8 copy.19
  313.7 23.0 %all-gather.24.cloned.1.call-done = bf16[4096,256]{1,0:T(8,128)(2,1)} async-done(((bf16[256,256]{1,0:T(8,128)(2,1)}), bf16[4096,256]{1,0:T(8,128)(2,1)}) %all-gather.24.cloned.1.call-update) | async-done | bytes 2097168 | tf_op jit(solution)/shard_map/all_gather | solution.py:108
  336.7 57.3 %all-gather.22.cloned.1.call-done = bf16[512,4096]{0,1:T(8,128)(2,1)} async-done(((bf16[512,256]{0,1:T(8,128)(2,1)}), bf16[512,4096]{0,1:T(8,128)(2,1)}) %all-gather.22.cloned.1.call-update) | async-done | bytes 4194320 | tf_op jit(solution)/shard_map/all_gather | solution.py:37
  394.0 4.9 %fusion.5 = bf16[512,1,256]{2,0,1:T(8,128)(2,1)} fusion(bf16[512,4096]{0,1:T(8,128)(2,1)} %all-gather.22.cloned.1.call-done, bf16[4096,256]{1,0:T(8,128)(2,1)} %all-gather.24.cloned.1.call-done), kind=kOutput, calls=%fused_computation.14 | convolution fusion | flops 1073872896 | bytes 6553600 | tf_op jit(solution)/shard_map/dot_general | solution.py:45
  398.9 36.7 %all-gather.26.cloned.1.call-done = bf16[4096,256]{1,0:T(8,128)(2,1)} async-done(((bf16[256,256]{1,0:T(8,128)(2,1)}), bf16[4096,256]{1,0:T(8,128)(2,1)}) %all-gather.26.cloned.1.call-update) | async-done | bytes 2097168 | tf_op jit(solution)/shard_map/all_gather | solution.py:109
  435.6 4.9 %fusion.6 = bf16[512,1,256]{2,0,1:T(8,128)(2,1)} fusion(bf16[512,4096]{0,1:T(8,128)(2,1)} %all-gather.22.cloned.1.call-done, bf16[4096,256]{1,0:T(8,128)(2,1)} %all-gather.26.cloned.1.call-done), kind=kOutput, calls=%fused_computation.15 | convolution fusion | flops 1073872896 | bytes 6553600 | tf_op jit(solution)/shard_map/dot_general | solution.py:45
  (22 shorter events, 0.2 us)
Async XLA Ops:
  7.2 8.3 %copy-start = (s32[2,256]{1,0:T(2,128)S(1)}, s32[2,256]{1,0:T(2,128)}, u32[]{:S(2)}) copy-start(s32[2,256]{1,0:T(2,128)} %param.11) | copy-start | bytes 6148
  7.2 46.3 %all-gather.14.cloned.1.call-start = ((), (), s32[]{:S(2)}) async-start(), calls=%async_computation.2 | async-start | bytes 2228224 | tf_op jit(solution)/shard_map/all_gather | solution.py:90
  7.9 104.3 %all-gather.10.cloned.1.call-start = ((), (), s32[]{:S(2)}) async-start(), calls=%async_computation | async-start | bytes 4456448 | tf_op jit(solution)/shard_map/all_gather | solution.py:32
  9.3 43.4 %copy-start.1 = (s32[2]{0:T(128)S(1)}, s32[2]{0:T(128)}, u32[]{:S(2)}) copy-start(s32[2]{0:T(128)} %param.12) | copy-start | bytes 28
  50.7 103.1 %all-gather.16.cloned.1.call-start = ((), (), s32[]{:S(2)}) async-start(), calls=%async_computation.3 | async-start | bytes 2228224 | tf_op jit(solution)/shard_map/all_gather | solution.py:91
  51.5 141.9 %all-gather.12.cloned.1.call-start = ((), (), s32[]{:S(2)}) async-start(), calls=%async_computation.1 | async-start | bytes 2228224 | tf_op jit(solution)/shard_map/all_gather | solution.py:92
  52.0 180.9 %all-gather.20.cloned.1.call-start = ((), (), s32[]{:S(2)}) async-start(), calls=%async_computation.5 | async-start | bytes 2228224 | tf_op jit(solution)/shard_map/all_gather | solution.py:102
  52.6 241.6 %all-gather.18.cloned.1.call-start = ((), (), s32[]{:S(2)}) async-start(), calls=%async_computation.4 | async-start | bytes 4456448 | tf_op jit(solution)/shard_map/all_gather | solution.py:101
  198.6 138.1 %all-gather.24.cloned.1.call-start = ((), (), s32[]{:S(2)}) async-start(), calls=%async_computation.7 | async-start | bytes 2228224 | tf_op jit(solution)/shard_map/all_gather | solution.py:108
  199.4 110.1 %copy-start.2 = (bf16[256]{0:T(256)(128)(2,1)S(1)}, bf16[256]{0:T(256)(128)(2,1)}, u32[]{:S(2)}) copy-start(bf16[256]{0:T(256)(128)(2,1)} %param.15) | copy-start | bytes 1540
  199.4 194.6 %all-gather.22.cloned.1.call-start = ((), (), s32[]{:S(2)}) async-start(), calls=%async_computation.6 | async-start | bytes 4456448 | tf_op jit(solution)/shard_map/all_gather | solution.py:37
  298.4 2.5 collective-permute-start
  300.9 3.9 collective-permute-start.1
  304.9 2.4 collective-permute-start.2
  307.3 3.9 collective-permute-start.3
  312.1 123.5 %all-gather.26.cloned.1.call-start = ((), (), s32[]{:S(2)}) async-start(), calls=%async_computation.8 | async-start | bytes 2228224 | tf_op jit(solution)/shard_map/all_gather | solution.py:109
Sparse Core Ops, SparseCore 0:
  9.8 43.6 all-gather.13
  56.5 55.7 all-gather.9
  114.1 39.7 all-gather.15
  155.5 37.8 all-gather.11
  195.1 37.8 all-gather.19
  235.7 58.4 all-gather.17
  296.0 40.6 all-gather.23
  339.7 54.2 all-gather.21
  395.9 39.7 all-gather.25
